TPU v7x, 32 devices: a whole 2x2x4 slice. The times are simulated.
32 devices in a mesh: grp: 2 (over y), prow: 4 (over z), pcol: 4 (over x, core).
Axes of the slice: x: 2, y: 2, z: 4, core: 2. Of those that a mesh axis runs over, the one named last changes fastest.
Arguments:
- eigvecs: float32 [8192, 4096], P(('grp', 'prow'), 'pcol'), parts along dimension 0, may hold values from -6 to 6
- y_panels: float32 [2, 8192, 256], P(None, ('grp', 'prow'), 'pcol'), parts along dimension 1, as said below
- t_factors: float32 [4, 256, 256], P('grp'), parts along dimension 0, as said below
Outputs:
- result: float32 [8192, 4096], P(('grp', 'prow'), 'pcol'), parts along dimension 0
There are 2 independent parts, one for each index of `grp`. A program takes and returns all parts, laid end to end along the dimension named above; each array names one. Nothing has to cross between parts.
Inputs may be any that keep to these rules, and one draw needn't show every extreme that they name: `y_panels`: column j of panel k is zero in rows above k * 256 + j and one in that row; t_factors[k] is upper triangular with diagonal between 0.5 and 1.5. Each t_factors[k] is upper triangular.
All inputs are finite; a program needn't handle non-finite values.
Results may differ from a plain program's by a relative error of at most 0.0001.
Values sent between devices are 32-bit elements; how exact they have to be, the bound alone decides.
No kernel may reach another device: no remote copies, remote signals or barrier semaphores. Data moves between devices by JAX's collectives and lax.ppermute only.
A program may use at most 64 MiB of HBM per device.

v0:
```python
import jax
import jax.numpy as jnp
from jax import lax
from jax.sharding import PartitionSpec as P


def update(current, vectors, triangle):
    highest = lax.Precision.HIGHEST
    local_sums = jnp.einsum("rc,rk->ck", current, vectors, precision=highest)
    sums = lax.psum(local_sums, "prow")
    scaled = jnp.einsum("ck,jk->cj", sums, triangle, precision=highest)
    return current - jnp.einsum("rj,cj->rc", vectors, scaled, precision=highest)


def per_device(eigvecs, y_panels, t_factors):
    gathered = lax.all_gather(y_panels, "pcol", axis=2, tiled=True)
    count = gathered.shape[0]
    current = eigvecs
    for index in reversed(range(count)):
        current = update(current, gathered[index], t_factors[index])
    return current


def solution(mesh):
    return jax.shard_map(
        per_device,
        mesh=mesh,
        in_specs=(
            P(("grp", "prow"), "pcol"),
            P(None, ("grp", "prow"), "pcol"),
            P("grp", None, None),
        ),
        out_specs=P(("grp", "prow"), "pcol"),
        check_vma=False,
    )
```

profile of v0, /device:TPU:0, one launch (start us, length us, event | category | flops | bytes accessed | tf_op | source)
XLA Modules:
  0.0 183.0 jit_solution(13575742015813939483)
XLA Ops:
  6.5 0.0 all-gather.2.cloned.1.call-start
  6.5 0.7 all-gather.2.cloned.1.call-update
  7.3 0.0 all-reduce.3.cloned.1.call-start
  7.3 26.9 %all-gather.2.cloned.1.call-done = f32[2,1024,256]{1,2,0:T(8,128)} async-done(((f32[2,1024,64]{1,2,0:T(8,128)}), f32[2,1024,256]{1,2,0:T(8,128)}) %all-gather.2.cloned.1.call-update) | async-done | bytes 2097168 | tf_op jit(solution)/shard_map/all_gather | solution.py:16
  34.2 10.1 %fusion = f32[1024,256]{1,0:T(8,128)} fusion(f32[1024,1024]{1,0:T(8,128)} %param.3, f32[2,1024,256]{1,2,0:T(8,128)} %all-gather.2.cloned.1.call-done), kind=kOutput, calls=%fused_computation.4 | convolution fusion | flops 3221225472 | bytes 6291456 | tf_op jit(solution)/shard_map/rc,rk->ck/dot_general | solution.py:9
  44.3 0.0 all-reduce.3.cloned.1.call-update
  44.4 0.0 copy-start.2
  44.4 0.0 copy-start.1
  44.4 0.2 all-reduce.5.cloned.1.call-start
  44.6 5.5 %copy.4 = f32[1024,1024]{0,1:T(8,128)} copy(f32[1024,1024]{1,0:T(8,128)} %param.3) | data formatting | bytes 8388608 | tf_op args[0]
  50.1 46.3 %all-reduce.3.cloned.1.call-done = f32[1024,256]{1,0:T(8,128)} async-done(((f32[1024,256]{1,0:T(8,128)}), f32[1024,256]{1,0:T(8,128)}) %all-reduce.3.cloned.1.call-update) | async-done | bytes 1048592 | tf_op jit(solution)/shard_map/psum | solution.py:10
  96.4 0.0 copy-done.2
  96.4 2.3 %fusion.4 = f32[1024,256]{1,0:T(8,128)S(1)} fusion(f32[1024,256]{1,0:T(8,128)} %all-reduce.3.cloned.1.call-done, f32[2,256,256]{2,1,0:T(8,128)S(1)} %copy-done.2), kind=kOutput, calls=%fused_computation.8 | convolution fusion | flops 805306368 | bytes 2359296 | tf_op jit(solution)/shard_map/ck,jk->cj/dot_general | solution.py:11
  98.7 0.0 copy-done.1
  98.7 5.7 %bitcast_subtract_fusion.1 = f32[1024,1024]{0,1:T(8,128)S(1)} fusion(f32[1024,1024]{0,1:T(8,128)} %copy.4, f32[1024,256]{1,0:T(8,128)S(1)} %fusion.4, f32[2,1024,256]{1,2,0:T(8,128)S(1)} %copy-done.1), kind=kOutput, calls=%fused_computation.1 | convolution fusion | flops 3222274048 | bytes 10485760 | tf_op jit(solution)/shard_map/rj,cj->rc/dot_general | solution.py:12
  104.4 0.0 copy-start
  104.4 2.0 %copy-done = f32[1024,1024]{0,1:T(8,128)} copy-done((f32[1024,1024]{0,1:T(8,128)}, f32[1024,1024]{0,1:T(8,128)S(1)}, u32[]{:S(2)}) %copy-start) | copy-done | bytes 4194328
  106.4 4.5 %fusion.1 = f32[1024,256]{1,0:T(8,128)} fusion(f32[1024,1024]{0,1:T(8,128)S(1)} %bitcast_subtract_fusion.1, f32[2,1024,256]{1,2,0:T(8,128)S(1)} %copy-done.1), kind=kOutput, calls=%fused_computation.5 | convolution fusion | flops 3221225472 | bytes 6291456 | tf_op jit(solution)/shard_map/rc,rk->ck/dot_general | solution.py:9
  110.9 0.0 all-reduce.5.cloned.1.call-update
  110.9 51.3 %all-reduce.5.cloned.1.call-done = f32[1024,256]{1,0:T(8,128)} async-done(((f32[1024,256]{1,0:T(8,128)}), f32[1024,256]{1,0:T(8,128)}) %all-reduce.5.cloned.1.call-update) | async-done | bytes 1048592 | tf_op jit(solution)/shard_map/psum | solution.py:10
  162.3 2.3 %fusion.2 = f32[1024,256]{1,0:T(8,128)S(1)} fusion(f32[1024,256]{1,0:T(8,128)} %all-reduce.5.cloned.1.call-done, f32[2,256,256]{2,1,0:T(8,128)S(1)} %copy-done.2), kind=kOutput, calls=%fused_computation.6 | convolution fusion | flops 805306368 | bytes 2359296 | tf_op jit(solution)/shard_map/ck,jk->cj/dot_general | solution.py:11
  164.5 6.6 %bitcast_subtract_fusion = f32[1024,1024]{0,1:T(8,128)} fusion(f32[1024,1024]{0,1:T(8,128)} %copy-done, f32[1024,256]{1,0:T(8,128)S(1)} %fusion.2, f32[2,1024,256]{1,2,0:T(8,128)S(1)} %copy-done.1), kind=kOutput, calls=%fused_computation | convolution fusion | flops 3222274048 | bytes 10485760 | tf_op jit(solution)/shard_map/rj,cj->rc/dot_general | solution.py:12
  171.1 5.3 %copy.5 = f32[1024,1024]{1,0:T(8,128)} copy(f32[1024,1024]{0,1:T(8,128)} %bitcast_subtract_fusion) | data formatting | bytes 8388608 | tf_op jit(solution)/shard_map/sub | solution.py:12
Async XLA Ops:
  6.5 27.7 %all-gather.2.cloned.1.call-start = ((), (), s32[]{:S(2)}) async-start(), calls=%async_computation | async-start | bytes 2621440 | tf_op jit(solution)/shard_map/all_gather | solution.py:16
  7.3 89.2 %all-reduce.3.cloned.1.call-start = ((), (), s32[]{:S(2)}) async-start(), calls=%async_computation.1 | async-start | bytes 2097152 | tf_op jit(solution)/shard_map/psum | solution.py:10
  44.4 52.1 %copy-start.2 = (f32[2,256,256]{2,1,0:T(8,128)S(1)}, f32[2,256,256]{2,1,0:T(8,128)}, u32[]{:S(2)}) copy-start(f32[2,256,256]{2,1,0:T(8,128)} %param.5) | copy-start | bytes 1572868
  44.4 54.3 %copy-start.1 = (f32[2,1024,256]{1,2,0:T(8,128)S(1)}, f32[2,1024,256]{1,2,0:T(8,128)}, u32[]{:S(2)}) copy-start(f32[2,1024,256]{1,2,0:T(8,128)} %all-gather.2.cloned.1.call-done) | copy-start | bytes 6291460
  44.4 117.9 %all-reduce.5.cloned.1.call-start = ((), (), s32[]{:S(2)}) async-start(), calls=%async_computation.2 | async-start | bytes 2097152 | tf_op jit(solution)/shard_map/psum | solution.py:10
  104.4 2.0 %copy-start = (f32[1024,1024]{0,1:T(8,128)}, f32[1024,1024]{0,1:T(8,128)S(1)}, u32[]{:S(2)}) copy-start(f32[1024,1024]{0,1:T(8,128)S(1)} %bitcast_subtract_fusion.1) | copy-start | bytes 12582916
Sparse Core Ops, SparseCore 0:
  8.9 25.2 all-gather.1
  44.5 51.8 all-reduce.2
  111.1 51.1 all-reduce.4
where the time goes:
time: 183 us
  waiting for transfers between devices  125 us (68%)
  matrix products  31.5 us (17%)
  between operations  13.2 us (7%)
  local copies, waits for them, and re-layouts  12.8 us (7%)
    psum x2, waiting for transfers between devices, update(): sums = lax.psum(local_sums, 'prow')  97.6 us
    all_gather x1, waiting for transfers between devices, per_device(): gathered = lax.all_gather(y_panels, 'pcol', axis=2, tiled=True)  26.9 us
    dot_general x2, matrix products, update(): local_sums = jnp.einsum('rc,rk->ck', current, vectors, precision=highest)  14.6 us
    dot_general x2, matrix products, update(): return current - jnp.einsum('rj,cj->rc', vectors, scaled, precision=highest)  12.3 us
    unnamed x7, local copies, waits for them, and re-layouts  7.5 us
    sub x1, local copies, waits for them, and re-layouts, update(): return current - jnp.einsum('rj,cj->rc', vectors, scaled, precision=highest)  5.34 us
    dot_general x2, matrix products, update(): scaled = jnp.einsum('ck,jk->cj', sums, triangle, precision=highest)  4.51 us
  transfers between devices with their start and end apart: 3, of which 3 were waited for; matrix products, arithmetic and copies ran while one was open for 3% of the time, Pallas kernels for 0%

commit v1 on v0

--- a/solution.py
+++ b/solution.py
@@ -7,7 +7,7 @@
 def update(current, vectors, triangle):
     highest = lax.Precision.HIGHEST
     local_sums = jnp.einsum("rc,rk->ck", current, vectors, precision=highest)
-    sums = lax.psum(local_sums, "prow")
+    sums = jnp.sum(lax.all_gather(local_sums, "prow"), axis=0)
     scaled = jnp.einsum("ck,jk->cj", sums, triangle, precision=highest)
     return current - jnp.einsum("rj,cj->rc", vectors, scaled, precision=highest)
 

time: 183 us -> 245 us (1.34)
  waiting for transfers between devices: 125 us -> 182 us
  other arithmetic: 0 us -> 5.19 us
    all_gather x0 -> x2, waiting for transfers between devices: none -> 155 us  [update(): sums = jnp.sum(lax.all_gather(local_sums, 'prow'), axis=0)]
    psum x2 -> x0, waiting for transfers between devices: 97.6 us -> none  [update(): sums = lax.psum(local_sums, 'prow')]
    reduce_sum x0 -> x2, other arithmetic: none -> 5.19 us  [update(): sums = jnp.sum(lax.all_gather(local_sums, 'prow'), axis=0)]
    unnamed x7 -> x5, local copies, waits for them, and re-layouts: 7.5 us -> 7.36 us
  transfers between devices with their start and end apart: 3 -> 3, of which waited for: 3 -> 3; matrix products, arithmetic and copies ran while one was open for 3% -> 2% of each run, Pallas kernels for 0% -> 0%
where the time goes in v1:
time: 245 us
  waiting for transfers between devices  182 us (74%)
  matrix products  30.9 us (13%)
  between operations  13.2 us (5%)
  local copies, waits for them, and re-layouts  12.7 us (5%)
  other arithmetic  5.19 us (2%)
    all_gather x2, waiting for transfers between devices, update(): sums = jnp.sum(lax.all_gather(local_sums, 'prow'), axis=0)  155 us
    all_gather x1, waiting for transfers between devices, per_device(): gathered = lax.all_gather(y_panels, 'pcol', axis=2, tiled=True)  26.9 us
    dot_general x2, matrix products, update(): local_sums = jnp.einsum('rc,rk->ck', current, vectors, precision=highest)  14.6 us
    dot_general x2, matrix products, update(): return current - jnp.einsum('rj,cj->rc', vectors, scaled, precision=highest)  12.3 us
    unnamed x5, local copies, waits for them, and re-layouts  7.36 us
    sub x1, local copies, waits for them, and re-layouts, update(): return current - jnp.einsum('rj,cj->rc', vectors, scaled, precision=highest)  5.34 us
    reduce_sum x2, other arithmetic, update(): sums = jnp.sum(lax.all_gather(local_sums, 'prow'), axis=0)  5.19 us
  transfers between devices with their start and end apart: 3, of which 3 were waited for; matrix products, arithmetic and copies ran while one was open for 2% of the time, Pallas kernels for 0%

profile of v1, /device:TPU:0, one launch (start us, length us, event | category | flops | bytes accessed | tf_op | source)
XLA Modules:
  0.0 244.5 jit_solution(6343151451239452119)
XLA Ops:
  6.5 0.0 all-gather.6.cloned.1.call-start
  6.5 0.7 all-gather.6.cloned.1.call-update
  7.3 0.0 all-gather.8.cloned.1.call-start
  7.3 26.9 %all-gather.6.cloned.1.call-done = f32[2,1024,256]{1,2,0:T(8,128)} async-done(((f32[2,1024,64]{1,2,0:T(8,128)}), f32[2,1024,256]{1,2,0:T(8,128)}) %all-gather.6.cloned.1.call-update) | async-done | bytes 2097168 | tf_op jit(solution)/shard_map/all_gather | solution.py:16
  34.2 10.1 %fusion = f32[1024,256]{1,0:T(8,128)} fusion(f32[1024,1024]{1,0:T(8,128)} %param.3, f32[2,1024,256]{1,2,0:T(8,128)} %all-gather.6.cloned.1.call-done), kind=kOutput, calls=%fused_computation.4 | convolution fusion | flops 3221225472 | bytes 6291456 | tf_op jit(solution)/shard_map/rc,rk->ck/dot_general | solution.py:9
  44.3 0.0 all-gather.8.cloned.1.call-update
  44.4 0.2 all-gather.10.cloned.1.call-start
  44.6 5.3 %copy.4 = f32[1024,1024]{0,1:T(8,128)} copy(f32[1024,1024]{1,0:T(8,128)} %param.3) | data formatting | bytes 8388608 | tf_op args[0]
  50.0 0.0 copy-start.1
  50.0 75.3 %all-gather.8.cloned.1.call-done = f32[4096,256]{1,0:T(8,128)} async-done(((f32[1024,256]{1,0:T(8,128)}), f32[4096,256]{1,0:T(8,128)}) %all-gather.8.cloned.1.call-update) | async-done | bytes 4194320 | tf_op jit(solution)/shard_map/all_gather | solution.py:10
  125.3 2.6 %reduce_sum.18 = f32[1024,256]{1,0:T(8,128)S(1)} reduce(f32[4,1024,256]{2,1,0:T(8,128)} %bitcast.26, f32[]{:T(128)} %constant.0.clone.1), dimensions={0}, to_apply=%region_0.0 | reduce | flops 786432 | bytes 5242884 | tf_op jit(solution)/shard_map/reduce_sum | solution.py:10
  127.9 2.0 fusion.4
  129.9 0.0 copy-done.1
  129.9 5.7 %bitcast_subtract_fusion.1 = f32[1024,1024]{0,1:T(8,128)S(1)} fusion(f32[1024,1024]{0,1:T(8,128)} %copy.4, f32[1024,256]{1,0:T(8,128)S(1)} %fusion.4, f32[2,1024,256]{1,2,0:T(8,128)S(1)} %copy-done.1), kind=kOutput, calls=%fused_computation.1 | convolution fusion | flops 3222274048 | bytes 10485760 | tf_op jit(solution)/shard_map/rj,cj->rc/dot_general | solution.py:12
  135.6 0.0 copy-start
  135.6 2.0 copy-done
  137.6 4.4 %fusion.1 = f32[1024,256]{1,0:T(8,128)} fusion(f32[1024,1024]{0,1:T(8,128)S(1)} %bitcast_subtract_fusion.1, f32[2,1024,256]{1,2,0:T(8,128)S(1)} %copy-done.1), kind=kOutput, calls=%fused_computation.5 | convolution fusion | flops 3221225472 | bytes 6291456 | tf_op jit(solution)/shard_map/rc,rk->ck/dot_general | solution.py:9
  142.0 0.0 all-gather.10.cloned.1.call-update
  142.0 79.4 %all-gather.10.cloned.1.call-done = f32[4096,256]{1,0:T(8,128)} async-done(((f32[1024,256]{1,0:T(8,128)}), f32[4096,256]{1,0:T(8,128)}) %all-gather.10.cloned.1.call-update) | async-done | bytes 4194320 | tf_op jit(solution)/shard_map/all_gather | solution.py:10
  221.4 2.6 %reduce_sum.19 = f32[1024,256]{1,0:T(8,128)S(1)} reduce(f32[4,1024,256]{2,1,0:T(8,128)} %bitcast.27, f32[]{:T(128)} %constant.0.clone.1), dimensions={0}, to_apply=%region_1.0 | reduce | flops 786432 | bytes 5242884 | tf_op jit(solution)/shard_map/reduce_sum | solution.py:10
  224.0 2.0 fusion.2
  226.0 6.6 %bitcast_subtract_fusion = f32[1024,1024]{0,1:T(8,128)} fusion(f32[1024,1024]{0,1:T(8,128)} %copy-done, f32[1024,256]{1,0:T(8,128)S(1)} %fusion.2, f32[2,1024,256]{1,2,0:T(8,128)S(1)} %copy-done.1), kind=kOutput, calls=%fused_computation | convolution fusion | flops 3222274048 | bytes 10485760 | tf_op jit(solution)/shard_map/rj,cj->rc/dot_general | solution.py:12
  232.6 5.3 %copy.5 = f32[1024,1024]{1,0:T(8,128)} copy(f32[1024,1024]{0,1:T(8,128)} %bitcast_subtract_fusion) | data formatting | bytes 8388608 | tf_op jit(solution)/shard_map/sub | solution.py:12
Async XLA Ops:
  6.5 27.7 %all-gather.6.cloned.1.call-start = ((), (), s32[]{:S(2)}) async-start(), calls=%async_computation | async-start | bytes 2621440 | tf_op jit(solution)/shard_map/all_gather | solution.py:16
  7.3 118.0 %all-gather.8.cloned.1.call-start = ((), (), s32[]{:S(2)}) async-start(), calls=%async_computation.1 | async-start | bytes 5242880 | tf_op jit(solution)/shard_map/all_gather | solution.py:10
  44.4 177.1 %all-gather.10.cloned.1.call-start = ((), (), s32[]{:S(2)}) async-start(), calls=%async_computation.2 | async-start | bytes 5242880 | tf_op jit(solution)/shard_map/all_gather | solution.py:10
  50.0 79.9 %copy-start.1 = (f32[2,1024,256]{1,2,0:T(8,128)S(1)}, f32[2,1024,256]{1,2,0:T(8,128)}, u32[]{:S(2)}) copy-start(f32[2,1024,256]{1,2,0:T(8,128)} %all-gather.6.cloned.1.call-done) | copy-start | bytes 6291460
  135.6 2.0 copy-start
Sparse Core Ops, SparseCore 0:
  8.9 25.2 all-gather.5
  44.5 80.7 all-gather.7
  142.2 79.2 all-gather.9
